TPU v7x, 32 devices: a whole 2x2x4 slice. The times are simulated.
32 devices in a mesh: shard: 4 (over z), ctx: 4 (over y, x), tp: 2 (over core).
Axes of the slice: x: 2, y: 2, z: 4, core: 2. Of those that a mesh axis runs over, the one named last changes fastest.
Arguments:
- tokens: bfloat16 [32, 1024, 768], P('shard', ('ctx', 'tp')), may hold values from -6 to 6
- project_weight: bfloat16 [768, 3, 768], P(('shard', 'ctx'), None, 'tp'), may hold values from -0.21875 to 0.21875
- attend_weight: bfloat16 [768, 768], P('tp', ('shard', 'ctx')), may hold values from -1.25 to 1.25
- up_weight: bfloat16 [768, 3072], P(('shard', 'ctx'), 'tp'), may hold values from -0.21875 to 0.21875
- down_weight: bfloat16 [3072, 768], P('tp', ('shard', 'ctx')), may hold values from -0.109375 to 0.109375
- project_bias: bfloat16 [3, 768], P(None, ('shard', 'ctx')), may hold values from -3 to 3
- attend_bias: bfloat16 [768], P(('shard', 'ctx')), may hold values from -3 to 3
- up_bias: bfloat16 [3072], P(('shard', 'ctx')), may hold values from -3 to 3
- down_bias: bfloat16 [768], P(('shard', 'ctx')), may hold values from -3 to 3
- first_gain: bfloat16 [768], P(('shard', 'ctx')), may hold values from 0.25 to 1.75
- first_shift: bfloat16 [768], P(('shard', 'ctx')), may hold values from -2 to 2
- second_gain: bfloat16 [768], P(('shard', 'ctx')), may hold values from 0.25 to 1.75
- second_shift: bfloat16 [768], P(('shard', 'ctx')), may hold values from -2 to 2
- segment_ids: int32 [32, 1024], P('shard'), may hold values from 0 to 63, never falling along the last dimension, each value on 1 to 512 neighbouring positions
- padding: int32 [32, 1024], P('shard'), may hold values 0 or 1
- cotangent: bfloat16 [32, 1024, 768], P('shard', ('ctx', 'tp')), may hold values from -6 to 6
Outputs:
- output: bfloat16 [32, 1024, 768], P('shard', ('ctx', 'tp'))
- tokens_grad: bfloat16 [32, 1024, 768], P('shard', ('ctx', 'tp'))
- project_weight_grad: float32 [768, 3, 768], P(('shard', 'ctx'), None, 'tp')
- attend_weight_grad: float32 [768, 768], P('tp', ('shard', 'ctx'))
- up_weight_grad: float32 [768, 3072], P(('shard', 'ctx'), 'tp')
- down_weight_grad: float32 [3072, 768], P('tp', ('shard', 'ctx'))
- project_bias_grad: float32 [3, 768], P(None, ('shard', 'ctx'))
- attend_bias_grad: float32 [768], P(('shard', 'ctx'))
- up_bias_grad: float32 [3072], P(('shard', 'ctx'))
- down_bias_grad: float32 [768], P(('shard', 'ctx'))
- first_gain_grad: float32 [768], P(('shard', 'ctx'))
- first_shift_grad: float32 [768], P(('shard', 'ctx'))
- second_gain_grad: float32 [768], P(('shard', 'ctx'))
- second_shift_grad: float32 [768], P(('shard', 'ctx'))
Inputs may be any that keep to these rules, and one draw needn't show every extreme that they name: `segment_ids`: segment numbers never fall along a sequence; a segment has 1 to 512 positions, and some segment of the draw has exactly 512.
All inputs are finite; a program needn't handle non-finite values. No bound on the sum of `padding` on one device may be relied on, other than what follows from the above.
Results may differ from a plain program's by a relative error of at most 0.02.
Values may be sent and summed in bfloat16 or wider, within the bound.
A program may use at most 320 MiB of HBM per device.

v0:
```python
import functools
import math

import jax
import jax.numpy as jnp
from jax import lax
from jax.experimental import pallas as pl
from jax.experimental.pallas import tpu as pltpu
from jax.sharding import PartitionSpec as P

D = 768
HEADS = 12
HEAD_DIM = 64
FF = 3072
S = 1024
LANES = 128
PAIRS = HEADS // 2
Q_ROWS = 128

HALF = D // 2
PACKED = 3 * HALF + LANES
RISE = FF // 2
UPPER = RISE + HALF

norm_eps = 1e-12
mask_fill = -1000000000.0

NT = (((1,), (1,)), ((), ()))
TN = (((0,), (0,)), ((), ()))
NN = (((1,), (0,)), ((), ()))


def dot(left, right, dims):
    return lax.dot_general(left, right, dims, preferred_element_type=jnp.float32)


def swap_pairs(values):
    lane = lax.broadcasted_iota(jnp.int32, values.shape, 1)
    width = values.shape[1]
    return jnp.where(
        lane % 2 == 0, -pltpu.roll(values, width - 1, 1), pltpu.roll(values, 1, 1)
    )


def turn(target, source):
    @pl.loop(0, source.shape[1] // LANES)
    def _(step):
        part = pl.ds(pl.multiple_of(step * LANES, LANES), LANES)
        target[part, :] = jnp.transpose(source[:, part])


def stack_heads(rows):
    lane = lax.broadcasted_iota(jnp.int32, rows.shape, 1)
    zero = jnp.zeros_like(rows)
    return jnp.concatenate(
        [jnp.where(lane < HEAD_DIM, rows, zero), jnp.where(lane < HEAD_DIM, zero, rows)], axis=0
    )


def pick_heads(both):
    return jnp.concatenate([both[:HEAD_DIM, :Q_ROWS], both[HEAD_DIM:, Q_ROWS:]], axis=0)


def spread_heads(row):
    return jnp.concatenate(
        [
            jnp.broadcast_to(row[:, :Q_ROWS], (HEAD_DIM, Q_ROWS)),
            jnp.broadcast_to(row[:, Q_ROWS:], (HEAD_DIM, Q_ROWS)),
        ],
        axis=0,
    )


def mask_bias(key_code, query_low, query_high):
    keys = jnp.broadcast_to(key_code, (key_code.shape[0], Q_ROWS))
    allowed = (keys >= query_low) & (keys <= query_high)
    return jnp.where(allowed, 0.0, mask_fill)


def stack_turned(turned):
    feature = lax.broadcasted_iota(jnp.int32, turned.shape, 0)
    zero = jnp.zeros_like(turned)
    return jnp.concatenate(
        [jnp.where(feature < HEAD_DIM, turned, zero), jnp.where(feature < HEAD_DIM, zero, turned)],
        axis=1,
    )


def twice(bias):
    return jnp.concatenate([bias, bias], axis=1)


def for_blocks(body, tick=None):
    @pl.loop(0, S // Q_ROWS)
    def _(block):
        if tick is not None:
            tick(block)
        body(block)


def packed(part, half):
    first = half * PACKED + part * HALF
    return slice(first, first + HALF)


def packed_weight(w_ref, part, half):
    return w_ref[..., packed(part, half)].reshape(D, HALF)


def project_rows(x_ref, w_ref, b_ref, cos_ref, sin_ref, q_ref, k_ref, v_ref):
    row_tile = 512

    @pl.loop(0, S // row_tile)
    def _(tile):
        rows = pl.ds(pl.multiple_of(tile * row_tile, row_tile), row_tile)
        x = x_ref[rows, :]
        cosine = cos_ref[rows, :]
        sine = sin_ref[rows, :]
        for part, out in enumerate((q_ref, k_ref, v_ref)):
            for pair in range(PAIRS):
                lanes = slice(pair * LANES, (pair + 1) * LANES)
                half, place = divmod(pair, PAIRS // 2)
                if place == 0:
                    joint = dot(x, packed_weight(w_ref, part, half), NN)
                piece = joint[:, place * LANES : (place + 1) * LANES] + b_ref[pl.ds(part, 1), lanes]
                if part < 2:
                    piece = piece * cosine + swap_pairs(piece) * sine
                if part == 0:
                    piece = piece.astype(jnp.bfloat16) * jnp.asarray(HEAD_DIM**-0.5, jnp.bfloat16)
                out[rows, lanes] = piece.astype(jnp.bfloat16)


def attend_kernel(
    x_ref, w_ref, b_ref, cos_ref, sin_ref, code_ref, low_ref, high_ref,
    q_ref, k_ref, v_ref, o_ref, lse_ref, *scratch,
):
    project_rows(x_ref, w_ref, b_ref, cos_ref, sin_ref, q_ref, k_ref, v_ref)
    attend_blocks(q_ref, k_ref, v_ref, o_ref, lse_ref, code_ref, low_ref, high_ref, *scratch)


def attend_scratch():
    return [
        pltpu.VMEM((D, S), jnp.bfloat16),
        pltpu.VMEM((D, S), jnp.bfloat16),
        pltpu.VMEM((S, Q_ROWS), jnp.float32),
        pltpu.VMEM((2, S, 2 * Q_ROWS), jnp.float32),
        pltpu.VMEM((2, S, 2 * Q_ROWS), jnp.bfloat16),
    ]


def attend_blocks(
    q_ref, k_ref, v_ref, o_ref, lse_ref, code_ref, low_ref, high_ref, q_turned, v_turned, bias, scores,
    probs, tick=None,
):
    turn(q_turned, q_ref)
    turn(v_turned, v_ref)

    def attend_block(block):
        rows = pl.ds(pl.multiple_of(block * Q_ROWS, Q_ROWS), Q_ROWS)
        bias[...] = mask_bias(code_ref[...], low_ref[:, rows], high_ref[:, rows])
        tops = {}

        def score(pair):
            lanes = slice(pair * LANES, (pair + 1) * LANES)
            raw = dot(k_ref[:, lanes], stack_turned(q_turned[lanes, rows]), NN)
            raw = raw + twice(bias[...])
            scores[pair % 2] = raw
            tops[pair] = jnp.max(raw, axis=0, keepdims=True)

        def mix(pair):
            lanes = slice(pair * LANES, (pair + 1) * LANES)
            expo = jnp.exp(scores[pair % 2] - tops[pair])
            probs[pair % 2] = expo.astype(jnp.bfloat16)
            total = jnp.sum(expo, axis=0, keepdims=True)
            mixed = dot(v_turned[lanes, :], probs[pair % 2], NN)
            out = pick_heads(mixed) / spread_heads(total)
            o_ref[rows, lanes] = jnp.transpose(out).astype(jnp.bfloat16)
            lse = tops[pair] + jnp.log(total)
            lse_ref[pl.ds(2 * pair, 1), rows] = lse[:, :Q_ROWS]
            lse_ref[pl.ds(2 * pair + 1, 1), rows] = lse[:, Q_ROWS:]

        score(0)
        for pair in range(PAIRS):
            if pair + 1 < PAIRS:
                score(pair + 1)
            mix(pair)

    for_blocks(attend_block, tick)


def attend_back_kernel(
    q_ref, k_ref, v_ref, o_ref, g_ref, lse_ref, cos_ref, sin_ref, code_ref, low_ref, high_ref,
    x_hbm, branch_hbm, w_hbm, given_ref, *rest,
):
    own = pl.program_id(0)
    attend_back_body(
        q_ref, k_ref, v_ref, o_ref, g_ref, lse_ref, cos_ref, sin_ref, code_ref, low_ref, high_ref,
        x_hbm.at[own], branch_hbm.at[own], w_hbm, given_ref, *rest,
    )


def attend_back_scratch():
    return [
        pltpu.VMEM((S, 3 * D), jnp.bfloat16),
        pltpu.VMEM((S, D), jnp.float32),
        pltpu.VMEM((S, D), jnp.float32),
        pltpu.VMEM((D, S), jnp.bfloat16),
        pltpu.VMEM((D, S), jnp.bfloat16),
        pltpu.VMEM((D, S), jnp.bfloat16),
        pltpu.VMEM((S, Q_ROWS), jnp.float32),
        pltpu.VMEM((2, S, 2 * Q_ROWS), jnp.bfloat16),
        pltpu.VMEM((2, S, 2 * Q_ROWS), jnp.bfloat16),
        pltpu.VMEM((S, D), jnp.bfloat16),
        pltpu.VMEM((S, D), jnp.bfloat16),
        pltpu.VMEM((D, 2 * PACKED), jnp.bfloat16),
        pltpu.VMEM((8, 3 * D), jnp.float32),
        pltpu.VMEM((LANES, D), jnp.float32),
        pltpu.SemaphoreType.DMA((3,)),
    ]


def attend_back_body(
    q_ref, k_ref, v_ref, o_ref, g_ref, lse_ref, cos_ref, sin_ref, code_ref, low_ref, high_ref,
    x_hbm, branch_hbm, w_hbm, given_ref, token_ref, weight_ref,
    joint_ref, keys_acc, values_acc, q_turned, k_turned, g_turned, bias, probs, score_grads,
    x_ref, branch_ref, w_ref, sums, vectors, sem, tick=None, after=None,
):
    loads = [
        pltpu.make_async_copy(source, target, sem.at[i])
        for i, (source, target) in enumerate(
            ((x_hbm, x_ref), (branch_hbm, branch_ref), (w_hbm, w_ref))
        )
    ]
    for load in loads:
        load.start()
    sums[...] = jnp.zeros_like(sums)
    keys_acc[...] = jnp.zeros_like(keys_acc)
    values_acc[...] = jnp.zeros_like(values_acc)
    turn(q_turned, q_ref)
    turn(k_turned, k_ref)
    turn(g_turned, g_ref)

    def keep(rows, lanes, grad):
        low = grad.astype(jnp.bfloat16)
        joint_ref[rows, lanes] = low
        sums[:, lanes] += jnp.sum(low.astype(jnp.float32).reshape(Q_ROWS // 8, 8, LANES), axis=0)

    def back_block(block):
        rows = pl.ds(pl.multiple_of(block * Q_ROWS, Q_ROWS), Q_ROWS)
        bias[...] = mask_bias(code_ref[...], low_ref[:, rows], high_ref[:, rows])
        cosine = cos_ref[rows, :]
        sine = sin_ref[rows, :]

        def slopes(pair):
            lanes = slice(pair * LANES, (pair + 1) * LANES)
            both = g_turned[lanes, rows].astype(jnp.float32) * jnp.transpose(
                o_ref[rows, lanes].astype(jnp.float32)
            )
            delta = jnp.concatenate(
                [
                    jnp.sum(both[:HEAD_DIM], axis=0, keepdims=True),
                    jnp.sum(both[HEAD_DIM:], axis=0, keepdims=True),
                ],
                axis=1,
            )
            level = jnp.concatenate(
                [lse_ref[pl.ds(2 * pair, 1), rows], lse_ref[pl.ds(2 * pair + 1, 1), rows]], axis=1
            )
            raw = dot(k_ref[:, lanes], stack_turned(q_turned[lanes, rows]), NN)
            prob = jnp.exp(raw + twice(bias[...]) - level)
            prob_grad = dot(v_ref[:, lanes], stack_turned(g_turned[lanes, rows]), NN)
            probs[pair % 2] = prob.astype(jnp.bfloat16)
            score_grads[pair % 2] = (prob * (prob_grad - delta)).astype(jnp.bfloat16)

        def gather(pair):
            lanes = slice(pair * LANES, (pair + 1) * LANES)
            values_acc[:, lanes] += dot(probs[pair % 2], stack_heads(g_ref[rows, lanes]), NN)
            keys_acc[:, lanes] += dot(
                score_grads[pair % 2], stack_heads(q_ref[rows, lanes]), NN
            )
            query = pick_heads(dot(k_turned[lanes, :], score_grads[pair % 2], NN))
            query = jnp.transpose(query) * (HEAD_DIM**-0.5)
            keep(rows, lanes, query * cosine - swap_pairs(query) * sine)

        slopes(0)
        for pair in range(PAIRS):
            if pair + 1 < PAIRS:
                slopes(pair + 1)
            gather(pair)

    for_blocks(back_block, tick)
    if after is not None:
        after()

    @pl.loop(0, S // Q_ROWS)
    def _(block):
        rows = pl.ds(pl.multiple_of(block * Q_ROWS, Q_ROWS), Q_ROWS)
        cosine = cos_ref[rows, :]
        sine = sin_ref[rows, :]
        for pair in range(PAIRS):
            lanes = slice(pair * LANES, (pair + 1) * LANES)
            key = keys_acc[rows, lanes]
            keep(
                rows,
                slice(D + pair * LANES, D + (pair + 1) * LANES),
                key * cosine - swap_pairs(key) * sine,
            )
            keep(
                rows,
                slice(2 * D + pair * LANES, 2 * D + (pair + 1) * LANES),
                values_acc[rows, lanes],
            )

    for load in loads:
        load.wait()
    turn(q_turned, x_ref)
    vectors[...] = jnp.zeros_like(vectors)
    vectors[: given_ref.shape[0], :] = given_ref[...]
    for part in range(3):
        columns = slice(part * D, (part + 1) * D)
        vectors[pl.ds(part, 1), :] = jnp.sum(sums[:, columns], axis=0, keepdims=True)

    def thirds(index):
        first = index % 2 * PACKED + index // 2 * HALF
        return (
            pl.ds(pl.multiple_of(index * HALF, LANES), HALF),
            pl.ds(pl.multiple_of(first, LANES), HALF),
        )

    keys_acc[...] = branch_ref[...].astype(jnp.float32)

    @pl.loop(0, 6)
    def _(index):
        plain, spread = thirds(index)
        grad = joint_ref[:, plain]
        weight_ref[:, spread] = dot(q_turned[...], grad, NN).astype(jnp.bfloat16)
        keys_acc[...] += dot(grad, w_ref[:, spread], NT)

    token_ref[...] = keys_acc[...].astype(jnp.bfloat16)
    turned = jnp.transpose(vectors[...]).astype(jnp.bfloat16)
    for half in range(2):
        weight_ref[:, half * PACKED + 3 * HALF : (half + 1) * PACKED] = turned


def whole(*shape):
    return pl.BlockSpec(shape, lambda i, *_: (0,) * len(shape))


def per(*shape):
    return pl.BlockSpec((None,) + shape, lambda i, *_: (i,) + (0,) * len(shape))


def attend(x, weight, bias, cosine, sine, code, low, high):
    own = x.shape[0]
    act = jax.ShapeDtypeStruct((own, S, D), jnp.bfloat16)
    return pl.pallas_call(
        attend_kernel,
        grid=(own,),
        in_specs=[
            per(S, D), whole(D, 2 * PACKED), whole(16, D), whole(S, LANES), whole(S, LANES),
            per(S, 1), per(1, S), per(1, S),
        ],
        out_specs=[per(S, D), per(S, D), per(S, D), per(S, D), per(HEADS, S)],
        scratch_shapes=attend_scratch(),
        out_shape=[act, act, act, act, jax.ShapeDtypeStruct((own, HEADS, S), jnp.float32)],
        compiler_params=pltpu.CompilerParams(vmem_limit_bytes=60 << 20),
        name="attend",
        cost_estimate=pl.CostEstimate(flops=6 * 10**9, bytes_accessed=12 << 20, transcendentals=6 << 20),
    )(x, weight, bias, cosine, sine, code, low, high)


def attend_back(q, k, v, o, g, lse, cosine, sine, code, low, high, x, branch_grad, weight, given):
    own = q.shape[0]
    hbm = pl.BlockSpec(memory_space=pl.ANY)
    return pl.pallas_call(
        attend_back_kernel,
        grid=(own,),
        in_specs=[
            per(S, D), per(S, D), per(S, D), per(S, D), per(S, D), per(HEADS, S),
            whole(S, LANES), whole(S, LANES), per(S, 1), per(1, S), per(1, S), hbm, hbm, hbm,
            per(16, D),
        ],
        out_specs=[per(S, D), per(D, 2 * PACKED)],
        scratch_shapes=attend_back_scratch(),
        out_shape=[
            jax.ShapeDtypeStruct((own, S, D), jnp.bfloat16),
            jax.ShapeDtypeStruct((own, D, 2 * PACKED), jnp.bfloat16),
        ],
        compiler_params=pltpu.CompilerParams(vmem_limit_bytes=60 << 20),
        name="attend_back",
        cost_estimate=pl.CostEstimate(flops=19 * 10**9, bytes_accessed=24 << 20, transcendentals=6 << 20),
    )(q, k, v, o, g, lse, cosine, sine, code, low, high, x, branch_grad, weight, given)


def mask_tables(segments, padding):
    code = 2 * segments + padding
    low = code
    high = 2 * segments + 1
    return code[:, :, None], low[:, None, :], high[:, None, :]


def angles():
    position = jnp.arange(S, dtype=jnp.int32).astype(jnp.float32)
    column = jnp.arange(LANES, dtype=jnp.int32) % HEAD_DIM // 2
    rate = jnp.exp(column.astype(jnp.float32) * (-2.0 * math.log(10000.0) / HEAD_DIM))
    phase = position[:, None] * rate[None, :]
    return jnp.cos(phase), jnp.sin(phase)


MESH = pl.DeviceIdType.MESH
ROWS = ("shard", "ctx")
EVERY = ("shard", "ctx", "tp")
SEQ = ("ctx", "tp")

BULK = ("upper", "down")
ITEMS = ("project",) + BULK
ROUTES = {"project": "zyx", "upper": "xyz", "down": "zxy"}
BEFORE = (('upper', None, 0), ('project', 1, None), ('project', 2, None), ('down', 1, None), ('project', 3, None), ('upper', None, 1), ('project', 4, None), ('down', 2, None), ('project', 5, None))
DURING = ((1, 'upper', None, 2), (3, 'down', 3, None), (6, 'down', 4, None))
AFTER = (('down', 5, None), ('upper', None, 3))
SUM_ROUTES = {"project": "xyz", "upper": "zyx", "down": "xzy"}


def places(depth):
    steps = [0]
    for k in range(1, depth):
        steps += [k, -k]
    return [(k, dy, dx) for k in steps for dy in (0, 1) for dx in (0, 1)]


def hops(place):
    return abs(place[0]) + place[1] + place[2]


def links(route, place, depth):
    apart = {"z": place[0] != 0, "y": place[1], "x": place[2]}
    level = max([i for i, axis in enumerate(route) if apart[axis]], default=-1)
    sign = (place[0] > 0) - (place[0] < 0)
    onward = []
    if level >= 0 and route[level] == "z" and abs(place[0]) + 1 < depth:
        onward.append(("z", -sign))
    for axis in route[level + 1 :]:
        onward += [("z", 1), ("z", -1)] if axis == "z" else [(axis, 1)]
    back = None if level < 0 else (route[level], sign if route[level] == "z" else 1)
    return back, onward


def seen_from(place, link):
    k, dy, dx = place
    axis, way = link
    return {"z": (k - way, dy, dx), "y": (k, 1 - dy, dx), "x": (k, dy, 1 - dx)}[axis]


class Here:
    def __init__(self):
        self.depth = lax.axis_size("shard")
        self.z = lax.axis_index("shard")
        self.c = lax.axis_index("ctx")
        self.t = lax.axis_index("tp")
        self.y = self.c // 2
        self.x = self.c % 2
        self.sides = lax.axis_size("tp")
        self.members = lax.axis_size("ctx") * self.sides
        self.rank = self.c * self.sides + self.t

    def rank_of(self, offset):
        return (self.rank + offset) % self.members

    def member(self, offset):
        rank = self.rank_of(offset)
        return (self.z, rank // self.sides, rank % self.sides)

    def device(self, link):
        axis, way = link
        if axis == "z":
            return (self.z + way, self.c, self.t)
        if axis == "y":
            return (self.z, 2 * (1 - self.y) + self.x, self.t)
        if axis == "x":
            return (self.z, 2 * self.y + (1 - self.x), self.t)
        return (self.z, self.c, 1 - self.t)

    def piece(self, place):
        k, dy, dx = place
        y = 1 - self.y if dy else self.y
        x = 1 - self.x if dx else self.x
        return (self.z + k) * 4 + 2 * y + x

    def inside(self, way):
        if way == 0:
            return None
        return self.z + way < self.depth if way > 0 else self.z + way >= 0

    def meet(self):
        barrier = pltpu.get_barrier_semaphore()
        for offset in range(1, self.members):
            pl.semaphore_signal(
                barrier, inc=1, device_id=self.member(offset), device_id_type=MESH
            )
        for way in (1, -1):

            @pl.when(self.inside(way))
            def _():
                pl.semaphore_signal(
                    barrier, inc=1, device_id=self.device(("z", way)), device_id_type=MESH
                )

        above = (self.z < self.depth - 1).astype(jnp.int32)
        below = (self.z > 0).astype(jnp.int32)
        pl.semaphore_wait(barrier, self.members - 1 + above + below)


class Exchange:
    def __init__(self, here, source, target, send_sem, recv_sem, own_sem):
        self.here, self.source, self.target = here, source, target
        self.send_sem, self.recv_sem, self.own_sem = send_sem, recv_sem, own_sem

    def block(self, ref, index):
        return ref.at[index] if len(ref.shape) == 3 else ref.at[rows_of(index)]

    def copy(self, offset):
        here = self.here
        return pltpu.make_async_remote_copy(
            src_ref=self.block(self.source, here.rank_of(offset)),
            dst_ref=self.block(self.target, here.rank),
            send_sem=self.send_sem.at[offset],
            recv_sem=self.recv_sem.at[offset],
            device_id=here.member(offset),
            device_id_type=MESH,
        )

    def arrival(self, offset):
        here = self.here
        landed = self.block(self.target, here.rank_of(here.members - offset))
        return pltpu.make_async_remote_copy(
            src_ref=landed,
            dst_ref=landed,
            send_sem=self.send_sem.at[offset],
            recv_sem=self.recv_sem.at[offset],
            device_id=here.member(offset),
            device_id_type=MESH,
        )

    def own(self):
        rank = self.here.rank
        return pltpu.make_async_copy(
            self.block(self.source, rank), self.block(self.target, rank), self.own_sem
        )

    def start(self):
        for offset in range(1, self.here.members):
            self.copy(offset).start()
        self.own().start()

    def receive(self):
        for offset in range(1, self.here.members):
            self.arrival(offset).wait_recv()
        self.own().wait()

    def drain(self):
        for offset in range(1, self.here.members):
            self.copy(offset).wait_send()


def rows_of(index):
    return pl.ds(pl.multiple_of(index * Q_ROWS, Q_ROWS), Q_ROWS)


def exchange_scratch(members):
    return [
        pltpu.SemaphoreType.DMA((members,)),
        pltpu.SemaphoreType.DMA((members,)),
        pltpu.SemaphoreType.DMA,
    ]


def guarded(condition, action):
    if condition is None:
        action()
    else:
        pl.when(condition)(action)


def columns(half, width):
    return pl.ds(pl.multiple_of(half * width, LANES), width)


def block_of(name, refs, piece, half, widths):
    return refs[name].at[piece, :, columns(half, widths[name])]


def gather_attend_kernel(
    widths, chip_count, project_hbm, upper_hbm, down_hbm, tokens_hbm,
    cos_ref, sin_ref, code_ref, low_ref, high_ref,
    q_ref, k_ref, v_ref, o_ref, lse_ref, wide_ref, project_out, x_out, upper_out, down_out,
    x_ref, w_ref, q_turned, v_turned, bias, scores, probs,
    send_sem, recv_sem, side_send, side_recv, own_sem, keep_sem, *exchange_sems,
):
    shards = dict(zip(ITEMS, (project_hbm, upper_hbm, down_hbm)))
    wholes = dict(zip(ITEMS, (w_ref, upper_out, down_out)))
    here = Here()
    tokens = Exchange(here, tokens_hbm, x_ref, *exchange_sems)
    spots = places(chip_count)
    order = sorted(spots, key=hops)
    home = (0, 0, 0)
    slot = {}
    for name in ITEMS:
        for place in spots:
            for link in links(ROUTES[name], place, chip_count)[1]:
                slot[name, place, link] = len(slot)

    def block(name, place, half):
        return block_of(name, wholes, here.piece(place), half, widths)

    def source(name, place, half):
        return shards[name] if place == home else block(name, place, half)

    def send(name, place, link):
        return pltpu.make_async_remote_copy(
            src_ref=source(name, place, here.t),
            dst_ref=block(name, place, here.t),
            send_sem=send_sem.at[slot[name, place, link]],
            recv_sem=recv_sem.at[ITEMS.index(name), spots.index(seen_from(place, link))],
            device_id=here.device(link),
            device_id_type=MESH,
        )

    def side(name, place, half):
        return pltpu.make_async_remote_copy(
            src_ref=source(name, place, half) if half is here.t else block(name, place, half),
            dst_ref=block(name, place, half),
            send_sem=side_send.at[ITEMS.index(name), spots.index(place)],
            recv_sem=side_recv.at[ITEMS.index(name), spots.index(place)],
            device_id=here.device(("tp", 1)),
            device_id_type=MESH,
        )

    def arrival(name, place):
        return pltpu.make_async_remote_copy(
            src_ref=block(name, place, here.t),
            dst_ref=block(name, place, here.t),
            send_sem=send_sem.at[0],
            recv_sem=recv_sem.at[ITEMS.index(name), spots.index(place)],
            device_id=here.device(("tp", 1)),
            device_id_type=MESH,
        )

    def own(name):
        return pltpu.make_async_copy(
            shards[name], block(name, home, here.t), own_sem.at[ITEMS.index(name)]
        )

    def relay(names, place):
        def pass_on():
            for name in names:
                if place != home:
                    arrival(name, place).wait_recv()
                for link in links(ROUTES[name], place, chip_count)[1]:
                    guarded(
                        here.inside(link[1]) if link[0] == "z" else None,
                        lambda name=name, link=link: send(name, place, link).start(),
                    )
                side(name, place, here.t).start()

        guarded(here.inside(place[0]), pass_on)

    def beside(names):
        for place in order:

            def wait(place=place):
                for name in names:
                    side(name, place, 1 - here.t).wait_recv()

            guarded(here.inside(place[0]), wait)

    def wave(name, far, near):
        for place in order[1:]:
            if (hops(place) == far if far is not None else abs(place[0]) == near):
                relay((name,), place)

    early = ITEMS[:1]
    here.meet()
    relay(ITEMS, home)
    tokens.start()
    for name in ITEMS:
        own(name).start()
    for stage in BEFORE:
        wave(*stage)
    own("project").wait()
    tokens.receive()
    beside(early)
    vectors = w_ref[:, :, 3 * HALF : PACKED].reshape(D, LANES).astype(jnp.float32)
    wide_ref[...] = jnp.transpose(vectors)[: wide_ref.shape[0]]
    keep = [
        pltpu.make_async_copy(w_ref, project_out, keep_sem.at[0]),
        pltpu.make_async_copy(x_ref, x_out, keep_sem.at[1]),
    ]
    for copy in keep:
        copy.start()
    project_rows(x_ref, w_ref, wide_ref, cos_ref, sin_ref, q_ref, k_ref, v_ref)

    def tick(step):
        for when, *stage in DURING:
            pl.when(step == when)(functools.partial(wave, *stage))

    attend_blocks(
        q_ref, k_ref, v_ref, o_ref, lse_ref, code_ref, low_ref, high_ref, q_turned, v_turned, bias,
        scores, probs, tick,
    )
    for stage in AFTER:
        wave(*stage)
    beside(BULK)
    for name in BULK:
        own(name).wait()
    tokens.drain()
    for copy in keep:
        copy.wait()
    for place in order:

        def finish(place=place):
            for name in ITEMS:
                side(name, place, here.t).wait_send()
                for link in links(ROUTES[name], place, chip_count)[1]:
                    guarded(
                        here.inside(link[1]) if link[0] == "z" else None,
                        lambda name=name, link=link: send(name, place, link).wait_send(),
                    )

        guarded(here.inside(place[0]), finish)


def link_count(depth):
    return sum(len(links(ROUTES[name], place, depth)[1]) for name in ITEMS for place in places(depth))


def gather_attend(shards, tokens, cosine, sine, code, low, high):
    chips, pieces = lax.axis_size("shard"), lax.axis_size("shard") * lax.axis_size("ctx")
    members = tokens.shape[0]
    widths = {name: shards[name].shape[-1] for name in ITEMS}
    depth = shards["upper"].shape[0]
    spots = len(places(chips))
    vmem, hbm = pl.BlockSpec(memory_space=pltpu.VMEM), pl.BlockSpec(memory_space=pl.ANY)

    def act(*shape):
        return jax.ShapeDtypeStruct(shape, jnp.bfloat16)

    def gathered(name):
        return act(pieces, depth, 2 * widths[name])

    per_place = pltpu.SemaphoreType.DMA((len(ITEMS), spots))
    outs = pl.pallas_call(
        functools.partial(gather_attend_kernel, widths, chips),
        out_shape=[
            act(S, D), act(S, D), act(S, D), act(S, D), jax.ShapeDtypeStruct((HEADS, S), jnp.float32),
            jax.ShapeDtypeStruct((16, D), jnp.float32), gathered("project"), act(S, D),
            gathered("upper"), gathered("down"),
        ],
        in_specs=[hbm] * 4 + [vmem] * 5,
        out_specs=[vmem] * 6 + [hbm] * 4,
        scratch_shapes=[
            pltpu.VMEM((S, D), jnp.bfloat16),
            pltpu.VMEM((pieces, depth, 2 * widths["project"]), jnp.bfloat16),
        ]
        + attend_scratch()
        + [
            pltpu.SemaphoreType.DMA((link_count(chips),)),
            per_place,
            per_place,
            per_place,
            pltpu.SemaphoreType.DMA((len(ITEMS),)),
            pltpu.SemaphoreType.DMA((2,)),
        ]
        + exchange_scratch(members),
        compiler_params=pltpu.CompilerParams(
            collective_id=0, has_side_effects=True, vmem_limit_bytes=60 << 20
        ),
        name="gather_attend",
    )(*[shards[name] for name in ITEMS], tokens, cosine, sine, code, low, high)
    query, key, value, attended, level, wide, project, x, upper, down = outs
    return query, key, value, attended, level, wide, x, dict(project=project, upper=upper, down=down)


def add_into(target, addend):
    height = 16

    @pl.loop(0, target.shape[0] // height)
    def _(step):
        rows = pl.ds(pl.multiple_of(step * height, height), height)
        total = target[rows, :].astype(jnp.float32) + addend[rows, :].astype(jnp.float32)
        target[rows, :] = total.astype(target.dtype)


class Sums:
    def __init__(self, here, names, routes, chip_count, widths, grads, mine, theirs, inbox, sems):
        self.here, self.names, self.routes, self.chip_count = here, names, routes, chip_count
        self.widths, self.grads, self.mine, self.theirs, self.inbox = widths, grads, mine, theirs, inbox
        self.load_sem, self.side_send, self.side_recv, self.send_sem, self.recv_sem = sems
        self.spots = places(chip_count)
        self.order = sorted(self.spots, key=hops, reverse=True)
        self.slot, self.box = {}, {}
        for name in names:
            local = 0
            for place in self.spots:
                for link in links(routes[name], place, chip_count)[1]:
                    self.slot[name, place, link] = len(self.slot)
                    self.box[name, place, link] = local
                    local += 1

    def at(self, name, place):
        return self.names.index(name), self.spots.index(place)

    def total(self, name, place):
        return self.mine[name].at[self.here.piece(place)]

    def other(self, name, place):
        return self.theirs[name].at[self.here.piece(place)]

    def load(self, name, place):
        source = block_of(name, self.grads, self.here.piece(place), self.here.t, self.widths)
        return pltpu.make_async_copy(
            source, self.total(name, place), self.load_sem.at[self.at(name, place)]
        )

    def side(self, name, place):
        here = self.here
        return pltpu.make_async_remote_copy(
            src_ref=block_of(name, self.grads, here.piece(place), 1 - here.t, self.widths),
            dst_ref=self.other(name, place),
            send_sem=self.side_send.at[self.at(name, place)],
            recv_sem=self.side_recv.at[self.at(name, place)],
            device_id=here.device(("tp", 1)),
            device_id_type=MESH,
        )

    def send(self, name, place, link):
        there = seen_from(place, link)
        back = (link[0], -link[1]) if link[0] == "z" else link
        return pltpu.make_async_remote_copy(
            src_ref=self.total(name, place),
            dst_ref=self.inbox[name].at[self.box[name, there, back]],
            send_sem=self.send_sem.at[self.at(name, place)],
            recv_sem=self.recv_sem.at[self.slot[name, there, back]],
            device_id=self.here.device(link),
            device_id_type=MESH,
        )

    def arrival(self, name, place, link):
        landed = self.inbox[name].at[self.box[name, place, link]]
        return pltpu.make_async_remote_copy(
            src_ref=landed,
            dst_ref=landed,
            send_sem=self.send_sem.at[0, 0],
            recv_sem=self.recv_sem.at[self.slot[name, place, link]],
            device_id=self.here.device(link),
            device_id_type=MESH,
        )

    def start(self):
        for place in self.order:

            def begin(place=place):
                for name in self.names:
                    self.side(name, place).start()
                    self.load(name, place).start()

            guarded(self.here.inside(place[0]), begin)

    def settle(self, distance):
        for place in self.order:
            if hops(place) != distance:
                continue

            def work(place=place):
                for name in self.names:
                    back, onward = links(self.routes[name], place, self.chip_count)
                    total = self.total(name, place)
                    self.load(name, place).wait()
                    self.side(name, place).wait_recv()
                    add_into(total, self.other(name, place))
                    for link in onward:

                        def take(link=link):
                            self.arrival(name, place, link).wait_recv()
                            add_into(total, self.inbox[name].at[self.box[name, place, link]])

                        guarded(self.here.inside(link[1]) if link[0] == "z" else None, take)
                    if back is not None:
                        self.send(name, place, back).start()

            guarded(self.here.inside(place[0]), work)

    def result(self, name):
        return self.total(name, (0, 0, 0))[...].astype(jnp.float32)

    def drain(self):
        for place in self.order:

            def finish(place=place):
                for name in self.names:
                    back, _ = links(self.routes[name], place, self.chip_count)
                    self.side(name, place).wait_send()
                    if back is not None:
                        self.send(name, place, back).wait_send()

            guarded(self.here.inside(place[0]), finish)


def sums_scratch(names, routes, chips, pieces, blocks, kinds):
    spots = places(chips)
    boxes = [sum(len(links(routes[name], place, chips)[1]) for place in spots) for name in names]
    per_place = pltpu.SemaphoreType.DMA((len(names), len(spots)))
    return (
        [pltpu.VMEM((pieces,) + block, kind) for block, kind in zip(blocks, kinds)] * 2
        + [pltpu.VMEM((box,) + block, kind) for box, block, kind in zip(boxes, blocks, kinds)]
        + [per_place] * 4
        + [pltpu.SemaphoreType.DMA((sum(boxes),))]
    )


def sums_of(here, names, routes, chip_count, widths, grads, refs):
    count = len(names)
    groups = [dict(zip(names, refs[i * count : (i + 1) * count])) for i in range(3)]
    return Sums(here, names, routes, chip_count, widths, grads, *groups, refs[3 * count :])


def back_scatter_kernel(
    widths, chip_count, *refs,
):
    body, bulk, outs = refs[:15], refs[15:17], refs[17:21]
    scratch = len(attend_back_scratch())
    local, rest = refs[21 : 21 + scratch], refs[21 + scratch :]
    here = Here()
    grads = dict(zip(BULK, bulk))
    sums = sums_of(here, BULK, SUM_ROUTES, chip_count, widths, grads, rest)
    here.meet()
    sums.start()
    farthest = max(hops(place) for place in sums.spots)
    steps = (1, 2, 3, 5, 7)

    def tick(step):
        for i, when in enumerate(steps):
            pl.when(step == when)(functools.partial(sums.settle, farthest - i))

    def after():
        for distance in range(farthest - len(steps), 0, -1):
            sums.settle(distance)

    attend_back_body(*body, *outs[:2], *local, tick=tick, after=after)
    sums.settle(0)
    for name, out in zip(BULK, outs[2:]):
        out[...] = sums.result(name)
    sums.drain()


def back_scatter(q, k, v, o, g, lse, cosine, sine, code, low, high, x, branch_grad, weight, given, grads):
    chips, pieces = lax.axis_size("shard"), lax.axis_size("shard") * lax.axis_size("ctx")
    vmem, hbm = pl.BlockSpec(memory_space=pltpu.VMEM), pl.BlockSpec(memory_space=pl.ANY)
    blocks = [(grads[name].shape[1], grads[name].shape[2] // 2) for name in BULK]
    widths = {name: block[-1] for name, block in zip(BULK, blocks)}
    outs = pl.pallas_call(
        functools.partial(back_scatter_kernel, widths, chips),
        out_shape=[
            jax.ShapeDtypeStruct((S, D), jnp.bfloat16),
            jax.ShapeDtypeStruct((D, 2 * PACKED), jnp.bfloat16),
        ]
        + [jax.ShapeDtypeStruct(block, jnp.float32) for block in blocks],
        in_specs=[vmem] * 11 + [hbm] * 3 + [vmem] + [hbm] * 2,
        out_specs=[vmem] * 4,
        scratch_shapes=attend_back_scratch()
        + sums_scratch(BULK, SUM_ROUTES, chips, pieces, blocks, [jnp.bfloat16] * len(BULK)),
        compiler_params=pltpu.CompilerParams(
            collective_id=3, has_side_effects=True, vmem_limit_bytes=67043328
        ),
        name="back_scatter",
    )(
        q, k, v, o, g, lse, cosine, sine, code, low, high, x, branch_grad, weight, given,
        *[grads[name] for name in BULK],
    )
    return outs[:2], dict(zip(BULK, outs[2:]))


LAST = ("project",)


def scatter_kernel(widths, chip_count, project_hbm, tokens_hbm, project_ref, tokens_out, *rest):
    here = Here()
    sums = sums_of(here, LAST, SUM_ROUTES, chip_count, widths, {"project": project_hbm}, rest[:-3])
    tokens = Exchange(here, tokens_hbm, tokens_out, *rest[-3:])
    here.meet()
    sums.start()
    farthest = max(hops(place) for place in sums.spots)
    for distance in range(farthest, -1, -1):
        sums.settle(distance)
        if distance == farthest - 1:
            tokens.start()
    project_ref[...] = sums.result("project")
    tokens.receive()
    tokens.drain()
    sums.drain()


def scatter_last(project, tokens_grad):
    chips, pieces = lax.axis_size("shard"), lax.axis_size("shard") * lax.axis_size("ctx")
    vmem, hbm = pl.BlockSpec(memory_space=pltpu.VMEM), pl.BlockSpec(memory_space=pl.ANY)
    block = (project.shape[1], project.shape[2] // 2)
    return pl.pallas_call(
        functools.partial(scatter_kernel, {"project": block[-1]}, chips),
        out_shape=[
            jax.ShapeDtypeStruct(block, jnp.float32),
            jax.ShapeDtypeStruct(tokens_grad.shape, tokens_grad.dtype),
        ],
        in_specs=[hbm] * 2,
        out_specs=[vmem, hbm],
        scratch_shapes=sums_scratch(LAST, SUM_ROUTES, chips, pieces, [block], [jnp.bfloat16])
        + exchange_scratch(tokens_grad.shape[0]),
        compiler_params=pltpu.CompilerParams(
            collective_id=1, has_side_effects=True, vmem_limit_bytes=60 << 20
        ),
        name="scatter_last",
    )(project, tokens_grad)


CHUNK = 512
STEP = 16
UNROLL = 4
ATTEND_BIAS, DOWN_BIAS, FIRST_GAIN, FIRST_SHIFT, SECOND_GAIN, SECOND_SHIFT = range(3, 9)
SUMS = 6


def row_mean(values):
    return jnp.sum(values, axis=-1, keepdims=True) * (1.0 / D)


def fold(values):
    return jnp.sum(values.reshape(values.shape[0] // 8, 8, values.shape[1]), axis=0)


def chunk_at(index):
    return pl.ds(pl.multiple_of(index * CHUNK, CHUNK), CHUNK)


def ffn_kernel(
    shared, a_ref, wide_ref, shift_ref, x_hbm, c_hbm, upper_hbm, down_hbm,
    joined_ref, branch_ref, sums_ref, up_sums_ref, out_hbm, upper_grad_hbm, down_grad_hbm,
    x_ref, c_ref, attend_ref, up_ref, down_ref, out_ref, hidden_ref, slope_ref, low_ref, ffn_ref, turned_ref,
    left, right, near, far, first, unit, acc, factor, sums, up_sums, stage, in_sem, out_sem, stage_sem,
    *exchange_sems,
):
    halves = [(half * UPPER, half * RISE, half * HALF) for half in range(2)]
    copies = [
        (upper_hbm.at[:, start + RISE : start + UPPER], attend_ref.at[:, low : low + HALF])
        for start, _, low in halves
    ]
    copies.append((x_hbm, x_ref))
    copies += [
        (upper_hbm.at[:, start : start + RISE], up_ref.at[:, rise : rise + RISE])
        for start, rise, _ in halves
    ]
    copies.append((down_hbm, down_ref))
    if not shared:
        copies.append((c_hbm, c_ref))
    loads = [
        pltpu.make_async_copy(source, target, in_sem.at[i]) for i, (source, target) in enumerate(copies)
    ]
    for load in loads:
        load.start()
    if shared:
        here = Here()
        barrier = pltpu.get_barrier_semaphore()
        for offset in range(1, here.members):
            pl.semaphore_signal(barrier, inc=1, device_id=here.member(offset), device_id_type=MESH)
        arriving = Exchange(here, c_hbm, c_ref, *exchange_sems[:3])
        leaving = Exchange(here, out_ref, out_hbm, *exchange_sems[3:])
    sums[...] = jnp.zeros_like(sums)
    up_sums[...] = jnp.zeros_like(up_sums)
    pairs = FF // CHUNK // 2

    def vector(index):
        return wide_ref[pl.ds(index, 1), :]

    def add_sum(index, values):
        sums[index - ATTEND_BIAS] += fold(values)

    def rows_loop(body):
        @pl.loop(0, S // STEP, unroll=UNROLL)
        def _(step):
            body(pl.ds(pl.multiple_of(step * STEP, STEP), STEP))

    loads[0].wait()
    loads[1].wait()
    acc[...] = dot(a_ref[...], attend_ref[...], NT)
    if shared:
        pl.semaphore_wait(barrier, here.members - 1)
        arriving.start()
    loads[2].wait()

    @rows_loop
    def _(rows):
        joined = x_ref[rows, :].astype(jnp.float32) + acc[rows, :] + vector(ATTEND_BIAS)
        centred = joined - row_mean(joined)
        scale = lax.rsqrt(row_mean(centred * centred) + norm_eps)
        normed = centred * scale
        unit[rows, :] = normed
        factor[rows, :] = scale
        result = normed * vector(FIRST_GAIN) + vector(FIRST_SHIFT)
        first[rows, :] = result
        low_ref[rows, :] = result.astype(jnp.bfloat16)

    for load in loads[3:6]:
        load.wait()

    def expand(target, index):
        target[...] = dot(low_ref[...], up_ref[:, chunk_at(index)], NN)

    def activate(source, target, index):
        pre = source[...] + shift_ref[:, chunk_at(index)]
        cumulative = 0.5 + 0.5 * lax.erf(pre * (1.0 / math.sqrt(2.0)))
        density = jnp.exp(-0.5 * pre * pre) * (1.0 / math.sqrt(2.0 * math.pi))
        hidden = (pre * cumulative).astype(jnp.bfloat16)
        target[...] = hidden
        hidden_ref[:, chunk_at(index)] = hidden
        slope_ref[:, chunk_at(index)] = (cumulative + pre * density).astype(jnp.bfloat16)

    def contract(source, index):
        acc[...] += dot(source[...], down_ref[:, chunk_at(index)], NT)

    def forward(pair):
        expand(right, 2 * pair + 1)
        activate(left, near, 2 * pair)
        expand(left, jnp.minimum(2 * pair + 2, 2 * pairs - 1))
        contract(near, 2 * pair)
        activate(right, far, 2 * pair + 1)
        contract(far, 2 * pair + 1)

    expand(left, 0)
    acc[...] = jnp.zeros_like(acc)

    pl.loop(0, pairs)(forward)
    if shared:
        arriving.receive()
    else:
        loads[6].wait()

    @rows_loop
    def _(rows):
        joined = first[rows, :] + acc[rows, :] + vector(DOWN_BIAS)
        centred = joined - row_mean(joined)
        scale = lax.rsqrt(row_mean(centred * centred) + norm_eps)
        normed = centred * scale
        out_ref[rows, :] = (normed * vector(SECOND_GAIN) + vector(SECOND_SHIFT)).astype(jnp.bfloat16)
        grad = c_ref[rows, :].astype(jnp.float32)
        add_sum(SECOND_GAIN, grad * normed)
        add_sum(SECOND_SHIFT, grad)
        inner = grad * vector(SECOND_GAIN)
        back = scale * (inner - row_mean(inner) - normed * row_mean(inner * normed))
        first[rows, :] = back
        low = back.astype(jnp.bfloat16)
        ffn_ref[rows, :] = low
        add_sum(DOWN_BIAS, low.astype(jnp.float32))

    if not shared:
        store = pltpu.make_async_copy(out_ref, out_hbm, out_sem)
        store.start()

    def stored(slot, target, index, spread):
        first = index * CHUNK + index // pairs * spread
        return pltpu.make_async_copy(
            stage.at[slot],
            target.at[:, pl.ds(pl.multiple_of(first, LANES), CHUNK)],
            stage_sem.at[slot],
        )

    def weight_grad(source, target, spread):
        @pl.loop(0, 2 * pairs)
        def _(index):
            slot = index % 2

            @pl.when(index > 1)
            def _():
                stored(slot, target, index, spread).wait()

            stage[slot] = dot(turned_ref[...], source[:, chunk_at(index)], NN).astype(jnp.bfloat16)
            stored(slot, target, index, spread).start()

        for slot in range(2):
            stored(slot, target, slot, spread).wait()

    turn(turned_ref, ffn_ref)
    if shared:
        leaving.start()
    weight_grad(hidden_ref, down_grad_hbm, 0)

    def widen(target, index):
        target[...] = dot(ffn_ref[...], down_ref[:, chunk_at(index)], NN)

    def reweigh(source, target, index):
        grad = (source[...] * slope_ref[:, chunk_at(index)].astype(jnp.float32)).astype(jnp.bfloat16)
        target[...] = grad
        hidden_ref[:, chunk_at(index)] = grad
        up_sums[:, chunk_at(index)] += fold(grad.astype(jnp.float32))

    def collect(source, index):
        acc[...] += dot(source[...], up_ref[:, chunk_at(index)], NT)

    def backward(pair):
        widen(right, 2 * pair + 1)
        reweigh(left, near, 2 * pair)
        widen(left, jnp.minimum(2 * pair + 2, 2 * pairs - 1))
        collect(near, 2 * pair)
        reweigh(right, far, 2 * pair + 1)
        collect(far, 2 * pair + 1)

    widen(left, 0)
    acc[...] = jnp.zeros_like(acc)

    pl.loop(0, pairs)(backward)

    @rows_loop
    def _(rows):
        grad = first[rows, :] + acc[rows, :]
        normed = unit[rows, :]
        add_sum(FIRST_GAIN, grad * normed)
        add_sum(FIRST_SHIFT, grad)
        inner = grad * vector(FIRST_GAIN)
        back = factor[rows, :] * (inner - row_mean(inner) - normed * row_mean(inner * normed))
        low = back.astype(jnp.bfloat16)
        branch_ref[rows, :] = low
        add_sum(ATTEND_BIAS, low.astype(jnp.float32))

    joined_ref[...] = dot(branch_ref[...], attend_ref[...], NN).astype(jnp.bfloat16)
    turn(turned_ref, low_ref)
    weight_grad(hidden_ref, upper_grad_hbm, HALF)
    turn(turned_ref, branch_ref)

    def attend_stored(slot):
        first = slot * UPPER + RISE
        return pltpu.make_async_copy(
            stage.at[slot, :, :HALF], upper_grad_hbm.at[:, first : first + HALF], stage_sem.at[slot]
        )

    for slot in range(2):
        stage[slot, :, :HALF] = dot(
            turned_ref[...], a_ref[:, slot * HALF : (slot + 1) * HALF], NN
        ).astype(jnp.bfloat16)
        attend_stored(slot).start()
    for index in range(SUMS):
        sums_ref[pl.ds(index, 1), :] = jnp.sum(sums[index], axis=0, keepdims=True)
    up_sums_ref[...] = jnp.sum(up_sums[...], axis=0, keepdims=True)
    for slot in range(2):
        attend_stored(slot).wait()
    if shared:
        leaving.receive()
        arriving.drain()
        leaving.drain()
    else:
        store.wait()


def feed_forward(attended, x, cotangent, upper, down_t, wide, up_shift, shared=False):
    vmem, hbm = pl.BlockSpec(memory_space=pltpu.VMEM), pl.BlockSpec(memory_space=pl.ANY)

    def low(*shape):
        return jax.ShapeDtypeStruct(shape, jnp.bfloat16)

    def full(*shape):
        return jax.ShapeDtypeStruct(shape, jnp.float32)

    def scratch(width, kind=jnp.bfloat16):
        return pltpu.VMEM((S, width), kind)

    return pl.pallas_call(
        functools.partial(ffn_kernel, shared),
        in_specs=[vmem] * 3 + [hbm] * 4,
        out_specs=[vmem] * 4 + [hbm] * 3,
        out_shape=[
            low(S, D), low(S, D), full(SUMS, D), full(1, FF), low(*cotangent.shape),
            low(D, 2 * UPPER), low(D, FF),
        ],
        scratch_shapes=[
            scratch(D), scratch(D), pltpu.VMEM((D, D), jnp.bfloat16), pltpu.VMEM((D, FF), jnp.bfloat16),
            pltpu.VMEM((D, FF), jnp.bfloat16),
            scratch(D), scratch(FF), scratch(FF), scratch(D), scratch(D), pltpu.VMEM((D, S), jnp.bfloat16),
            scratch(CHUNK, jnp.float32), scratch(CHUNK, jnp.float32), scratch(CHUNK), scratch(CHUNK),
            scratch(D, jnp.float32), scratch(D, jnp.float32), scratch(D, jnp.float32),
            scratch(1, jnp.float32),
            pltpu.VMEM((SUMS, 8, D), jnp.float32), pltpu.VMEM((8, FF), jnp.float32),
            pltpu.VMEM((2, D, CHUNK), jnp.bfloat16),
            pltpu.SemaphoreType.DMA((7,)), pltpu.SemaphoreType.DMA, pltpu.SemaphoreType.DMA((2,)),
        ]
        + 2 * (exchange_scratch(cotangent.shape[0]) if shared else []),
        compiler_params=pltpu.CompilerParams(
            vmem_limit_bytes=63 << 20,
            collective_id=2 if shared else None,
            has_side_effects=shared,
        ),
        name="feed_forward",
        cost_estimate=pl.CostEstimate(
            flops=6 * S * D * (D + 2 * FF), bytes_accessed=30 << 20, transcendentals=2 * S * FF
        ),
    )(attended, wide, up_shift.reshape(1, FF), x, cotangent, upper, down_t)


def fitting(shards, own):
    return own == 1 and lax.axis_size("ctx") == 4 and lax.axis_size("tp") == 2 and shards["upper"].shape[0] % 16 == 0


def gather_plain(shards):
    return {
        name: lax.all_gather(
            lax.all_gather(shards[name], ROWS, axis=0), "tp", axis=2, tiled=True
        )
        for name in ITEMS
    }


def scatter_plain(grads):
    shards = {}
    for name in ITEMS:
        part = lax.psum_scatter(grads[name], "tp", scatter_dimension=2, tiled=True)
        part = lax.psum_scatter(part, ROWS, scatter_dimension=0, tiled=False)
        shards[name] = part.astype(jnp.float32)
    return shards


def local(
    tokens, project_weight, attend_weight, up_weight, down_weight, project_bias, attend_bias,
    up_bias, down_bias, first_gain, first_shift, second_gain, second_shift, segment_ids, padding,
    cotangent,
):
    seq_count = tokens.shape[0]
    members = lax.axis_size("ctx") * lax.axis_size("tp")
    own = seq_count // members
    rank = lax.axis_index("ctx") * lax.axis_size("tp") + lax.axis_index("tp")
    pieces = lax.axis_size("shard") * lax.axis_size("ctx")
    depth = D // pieces

    def to_sequences(array):
        parts = array.reshape((members, own) + array.shape[1:])
        parts = lax.all_to_all(parts, SEQ, 0, 0, tiled=True)
        return jnp.swapaxes(parts, 0, 1).reshape(own, S, D)

    def to_blocks(array):
        parts = jnp.swapaxes(array.reshape(own, members, S // members, D), 0, 1)
        return lax.all_to_all(parts, SEQ, 0, 0, tiled=True).reshape(tokens.shape)

    segments = lax.dynamic_slice_in_dim(segment_ids, rank * own, own, 0)
    pads = lax.dynamic_slice_in_dim(padding, rank * own, own, 0)

    vectors = jnp.concatenate(
        [
            project_bias,
            attend_bias[None],
            down_bias[None],
            first_gain[None],
            first_shift[None],
            second_gain[None],
            second_shift[None],
            up_bias.reshape(FF // D, depth),
        ],
        axis=0,
    )
    shards = {
        "project": jnp.concatenate(
            [
                project_weight.reshape(depth, 3 * HALF),
                jnp.pad(jnp.transpose(vectors), ((0, 0), (0, LANES - vectors.shape[0]))),
            ],
            axis=1,
        ),
        "upper": jnp.concatenate([up_weight, jnp.transpose(attend_weight)], axis=1),
        "down": jnp.transpose(down_weight),
    }
    custom = fitting(shards, own)
    tables = mask_tables(segments, pads)
    cosine, sine = angles()
    if custom:
        *saved, wide, x, wholes = gather_attend(
            shards, tokens, cosine, sine, *[table[0] for table in tables]
        )
        query, key, value, attended, level, x = [array[None] for array in saved + [x]]
    else:
        wholes, x = gather_plain(shards), to_sequences(tokens)
    project = wholes["project"].reshape(D, 2 * PACKED)
    upper = wholes["upper"].reshape(D, 2 * UPPER)
    down_t = wholes["down"].reshape(D, FF)
    if not custom:
        wide = jnp.transpose(project[:, 3 * HALF : 3 * HALF + 16]).astype(jnp.float32)
        query, key, value, attended, level = attend(x, project, wide, cosine, sine, *tables)
    up_shift = jnp.swapaxes(wide[9:13].reshape(FF // D, pieces, depth), 0, 1).reshape(FF)
    params = (upper, down_t, wide, up_shift)
    if custom:
        parts = [feed_forward(attended[0], x[0], cotangent, *params, shared=True)]
    else:
        incoming = to_sequences(cotangent)
        parts = [feed_forward(attended[i], x[i], incoming[i], *params) for i in range(own)]
    attended_grad = jnp.stack([part[0] for part in parts])
    branch_grad = jnp.stack([part[1] for part in parts])
    sums = sum(part[2] for part in parts)
    up_bias_grad = sum(part[3] for part in parts)
    output = parts[0][4] if custom else to_blocks(jnp.stack([part[4] for part in parts]))
    upper_grad, down_grad = (
        parts[0][k] if own == 1 else sum(part[k].astype(jnp.float32) for part in parts).astype(jnp.bfloat16)
        for k in (5, 6)
    )
    up_bias_grad = jnp.swapaxes(up_bias_grad.reshape(pieces, FF // D, depth), 0, 1).reshape(FF // D, D)
    given = jnp.concatenate([jnp.zeros((3, D), jnp.float32), sums, up_bias_grad, jnp.zeros((3, D), jnp.float32)])
    grads = {
        "upper": upper_grad.reshape(pieces, depth, 2 * UPPER),
        "down": down_grad.reshape(pieces, depth, FF),
    }
    inputs = (query, key, value, attended, attended_grad, level)
    if custom:
        (tokens_grad, project_grad), shards = back_scatter(
            *[array[0] for array in inputs], cosine, sine, *[table[0] for table in tables], x[0],
            branch_grad[0], project, given, grads,
        )
        shards["project"], tokens_grad = scatter_last(
            project_grad.reshape(pieces, depth, 2 * PACKED), tokens_grad.reshape(tokens.shape)
        )
    else:
        given = jnp.concatenate([given[None], jnp.zeros((own - 1,) + given.shape, jnp.float32)])
        tokens_grad, project_grad = attend_back(
            *inputs, cosine, sine, *tables, x, branch_grad, project, given
        )
        project_grad = jnp.sum(project_grad.astype(jnp.float32), axis=0).astype(jnp.bfloat16)
        grads["project"] = project_grad.reshape(pieces, depth, 2 * PACKED)
        shards, tokens_grad = scatter_plain(grads), to_blocks(tokens_grad)
    sums = jnp.transpose(shards["project"][:, 3 * HALF : 3 * HALF + 13])
    return (
        output,
        tokens_grad,
        shards["project"][:, : 3 * HALF].reshape(depth, 3, HALF),
        jnp.transpose(shards["upper"][:, RISE:]),
        shards["upper"][:, :RISE],
        jnp.transpose(shards["down"]),
        sums[:3],
        sums[3],
        sums[9:].reshape(-1),
        sums[4],
        sums[5],
        sums[6],
        sums[7],
        sums[8],
    )


def solution(mesh):
    in_specs = (
        P("shard", ("ctx", "tp"), None),
        P(("shard", "ctx"), None, "tp"),
        P("tp", ("shard", "ctx")),
        P(("shard", "ctx"), "tp"),
        P("tp", ("shard", "ctx")),
        P(None, ("shard", "ctx")),
        P(("shard", "ctx")),
        P(("shard", "ctx")),
        P(("shard", "ctx")),
        P(("shard", "ctx")),
        P(("shard", "ctx")),
        P(("shard", "ctx")),
        P(("shard", "ctx")),
        P("shard", None),
        P("shard", None),
        P("shard", ("ctx", "tp"), None),
    )
    out_specs = (
        P("shard", ("ctx", "tp"), None),
        P("shard", ("ctx", "tp"), None),
        P(("shard", "ctx"), None, "tp"),
        P("tp", ("shard", "ctx")),
        P(("shard", "ctx"), "tp"),
        P("tp", ("shard", "ctx")),
        P(None, ("shard", "ctx")),
        P(("shard", "ctx")),
        P(("shard", "ctx")),
        P(("shard", "ctx")),
        P(("shard", "ctx")),
        P(("shard", "ctx")),
        P(("shard", "ctx")),
        P(("shard", "ctx")),
    )
    return jax.shard_map(local, mesh=mesh, in_specs=in_specs, out_specs=out_specs, check_vma=False)
```

profile of v0, /device:TPU:0, one launch (start us, length us, event | category | flops | bytes accessed | tf_op | source)
XLA Modules:
  0.0 321.4 jit_solution(7640291542233102045)
XLA Ops:
  0.8 1.5 broadcast_add_fusion
  2.3 1.0 copy.60.code_ref.refs_8_
  3.3 3.1 multiply_sine_fusion
  6.7 0.7 fusion.1.project_hbm
  7.4 0.7 pad_maximum_fusion.upper_hbm
  8.1 102.9 %gather_attend.1 = (bf16[1024,768]{1,0:T(8,128)(2,1)}, bf16[1024,768]{1,0:T(8,128)(2,1)}, bf16[1024,768]{1,0:T(8,128)(2,1)}, bf16[1024,768]{1,0:T(8,128)(2,1)}, ...) custom-call(bf16[48,1280]{1,0:T(8,128)(2,1)} %fusion.1.project_hbm, ...), custom_call_target="tpu_custom_call" | custom-call | tf_op jit(solution)/shard_map/gather_attend/pallas_call | solution.py:751
  111.0 0.7 slice.39
  111.8 0.7 reshape_reshape.3.shift_ref
  112.6 75.3 %feed_forward.1 = (bf16[1024,768]{1,0:T(8,128)(2,1)}, bf16[1024,768]{1,0:T(8,128)(2,1)}, f32[6,768]{1,0:T(8,128)}, f32[1,3072]{1,0:T(1,128)}, bf16[8,128,768]{2,...) custom-call(bf16[1024,768]{1,0:T(8,128)(2,1)} %get-tuple-element.37.a_ref.refs_3_, ...), custom_call_target="tpu_custom_call" | custom-call | flops 32614907904 | bytes 31457280 | tf_op jit(solution)/shard_map/feed_forward/pallas_call | solution.py:1271
  188.4 1.4 reduce.15
  190.0 1.4 pad_maximum_fusion.1.refs_14_
  191.4 76.7 %back_scatter.1 = (bf16[1024,768]{1,0:T(8,128)(2,1)}, bf16[768,2560]{1,0:T(8,128)(2,1)}, f32[48,1920]{1,0:T(8,128)}, f32[48,1536]{1,0:T(8,128)}) custom-call(bf16[1024,768]{1,0:T(8,128)(2,1)} %get-tuple-element.43.refs_0_, bf16[1024,768]{1,0:T(8,128)(2,1)} %get-tuple-element.44.refs_1_, bf16[1024,768]{1,0:T(8,128)(2,1)} %get-tuple-element.45.refs_2_, ...), custom_call_target="tpu_custom_call" | custom-call | tf_op jit(solution)/shard_map/back_scatter/pallas_call | solution.py:960
  268.1 43.3 %scatter_last.1 = (f32[48,1280]{1,0:T(8,128)}, bf16[8,128,768]{2,1,0:T(8,128)(2,1)}) custom-call(bf16[16,48,2560]{2,1,0:T(8,128)(2,1)} %bitcast.38, bf16[8,128,768]{2,1,0:T(8,128)(2,1)} %bitcast.40), custom_call_target="tpu_custom_call" | custom-call | tf_op jit(solution)/shard_map/scatter_last/pallas_call | solution.py:1006
  311.4 1.1 slice.40
  312.5 0.7 copy.72
  313.2 0.7 slice_bitcast_fusion.1
  314.1 0.7 reshape.114
  314.8 0.8 slice_reduce_fusion
  315.5 0.7 copy.66
  316.2 0.7 slice.42
  317.6 1.1 copy.78
  318.7 0.8 copy-done.1
  319.6 1.1 copy.79
  320.7 0.7 copy.80
  (47 shorter events, 1.9 us)
Async XLA Ops:
  0.7 5.7 %copy-start.5 = (bf16[48,3,384]{2,0,1:T(8,128)(2,1)S(1)}, bf16[48,3,384]{2,0,1:T(8,128)(2,1)}, u32[]{:S(2)}) copy-start(bf16[48,3,384]{2,0,1:T(8,128)(2,1)} %param.17) | copy-start | bytes 331780
  0.7 5.7 %copy-start.15 = (bf16[192]{0:T(256)(128)(2,1)S(1)}, bf16[192]{0:T(256)(128)(2,1)}, u32[]{:S(2)}) copy-start(bf16[192]{0:T(256)(128)(2,1)} %param.23) | copy-start | bytes 1156
  0.7 5.8 %copy-start.9 = (bf16[48]{0:T(256)(128)(2,1)S(1)}, bf16[48]{0:T(256)(128)(2,1)}, u32[]{:S(2)}) copy-start(bf16[48]{0:T(256)(128)(2,1)} %param.22) | copy-start | bytes 292
  0.7 5.8 %copy-start.10 = (bf16[48]{0:T(256)(128)(2,1)S(1)}, bf16[48]{0:T(256)(128)(2,1)}, u32[]{:S(2)}) copy-start(bf16[48]{0:T(256)(128)(2,1)} %param.24) | copy-start | bytes 292
  0.7 5.8 %copy-start.11 = (bf16[48]{0:T(256)(128)(2,1)S(1)}, bf16[48]{0:T(256)(128)(2,1)}, u32[]{:S(2)}) copy-start(bf16[48]{0:T(256)(128)(2,1)} %param.25) | copy-start | bytes 292
  0.7 5.8 %copy-start.12 = (bf16[48]{0:T(256)(128)(2,1)S(1)}, bf16[48]{0:T(256)(128)(2,1)}, u32[]{:S(2)}) copy-start(bf16[48]{0:T(256)(128)(2,1)} %param.26) | copy-start | bytes 292
  0.7 5.8 %copy-start.13 = (bf16[48]{0:T(256)(128)(2,1)S(1)}, bf16[48]{0:T(256)(128)(2,1)}, u32[]{:S(2)}) copy-start(bf16[48]{0:T(256)(128)(2,1)} %param.27) | copy-start | bytes 292
  0.7 5.8 %copy-start.14 = (bf16[48]{0:T(256)(128)(2,1)S(1)}, bf16[48]{0:T(256)(128)(2,1)}, u32[]{:S(2)}) copy-start(bf16[48]{0:T(256)(128)(2,1)} %param.28) | copy-start | bytes 292
  0.7 5.8 %copy-start.8 = (bf16[3,48]{1,0:T(4,128)(2,1)S(1)}, bf16[3,48]{1,0:T(4,128)(2,1)}, u32[]{:S(2)}) copy-start(bf16[3,48]{1,0:T(4,128)(2,1)} %param.21) | copy-start | bytes 868
  0.7 6.6 %copy-start.7 = (bf16[384,48]{0,1:T(8,128)(2,1)S(1)}, bf16[384,48]{0,1:T(8,128)(2,1)}, u32[]{:S(2)}) copy-start(bf16[384,48]{0,1:T(8,128)(2,1)} %param.18) | copy-start | bytes 110596
  0.8 6.6 %copy-start.4 = (bf16[48,1536]{1,0:T(8,128)(2,1)S(1)}, bf16[48,1536]{1,0:T(8,128)(2,1)}, u32[]{:S(2)}) copy-start(bf16[48,1536]{1,0:T(8,128)(2,1)} %param.19) | copy-start | bytes 442372
  2.3 5.8 %copy-start.6 = (s32[1,1024]{1,0:T(1,128)}, s32[1,1024]{1,0:T(1,128)S(1)}, u32[]{:S(2)}) copy-start(s32[1,1024]{1,0:T(1,128)S(1)} %get-tuple-element.109.low_ref.refs_9_) | copy-start | bytes 12292
  268.1 48.1 %copy-start.2 = (f32[48,1920]{1,0:T(8,128)S(1)}, f32[48,1920]{1,0:T(8,128)}, u32[]{:S(2)}) copy-start(f32[48,1920]{1,0:T(8,128)} %get-tuple-element.58) | copy-start | bytes 1105924
  311.4 6.2 %copy-start = (bf16[8,128,768]{2,1,0:T(8,128)(2,1)S(1)}, bf16[8,128,768]{2,1,0:T(8,128)(2,1)}, u32[]{:S(2)}) copy-start(bf16[8,128,768]{2,1,0:T(8,128)(2,1)} %get-tuple-element.126) | copy-start | bytes 4718596
  317.6 2.0 copy-start.1
  319.6 1.1 copy-start.3
where the time goes:
time: 322 us; the launch traced here: 321 us
  Pallas kernels  298 us (93%)
  local copies, waits for them, and re-layouts  13.6 us (4%)
  other arithmetic  8.69 us (3%)
    pallas_call x1, Pallas kernels, gather_attend(): pl.pallas_call(functools.partial(gather_attend_kernel, widths, chips), ou...  103 us
    pallas_call x1, Pallas kernels, back_scatter(): pl.pallas_call(functools.partial(back_scatter_kernel, widths, chips), out...  76.7 us
    pallas_call x1, Pallas kernels, feed_forward(): pl.pallas_call(functools.partial(ffn_kernel, shared), in_specs=[vmem] * 3...  75.3 us
    pallas_call x1, Pallas kernels, scatter_last(): pl.pallas_call(functools.partial(scatter_kernel, {'project': block[-1]},...  43.3 us

commit v1 on v0

--- a/solution.py
+++ b/solution.py
@@ -418,7 +418,7 @@
 BEFORE = (('upper', None, 0), ('project', 1, None), ('project', 2, None), ('down', 1, None), ('project', 3, None), ('upper', None, 1), ('project', 4, None), ('down', 2, None), ('project', 5, None))
 DURING = ((1, 'upper', None, 2), (3, 'down', 3, None), (6, 'down', 4, None))
 AFTER = (('down', 5, None), ('upper', None, 3))
-SUM_ROUTES = {"project": "xyz", "upper": "zyx", "down": "xzy"}
+SUM_ROUTES = {"project": "xyz", "upper": "zyx", "down": "zxy"}
 
 
 def places(depth):

time: 322 us -> 325 us (level)
  no operation moved by 1% of the time
where the time goes in v1:
time: 325 us; the launch traced here: 324 us
  Pallas kernels  301 us (93%)
  local copies, waits for them, and re-layouts  13.6 us (4%)
  other arithmetic  8.69 us (3%)
    pallas_call x1, Pallas kernels, gather_attend(): pl.pallas_call(functools.partial(gather_attend_kernel, widths, chips), ou...  103 us
    pallas_call x1, Pallas kernels, back_scatter(): pl.pallas_call(functools.partial(back_scatter_kernel, widths, chips), out...  79.7 us
    pallas_call x1, Pallas kernels, feed_forward(): pl.pallas_call(functools.partial(ffn_kernel, shared), in_specs=[vmem] * 3...  75.3 us
    pallas_call x1, Pallas kernels, scatter_last(): pl.pallas_call(functools.partial(scatter_kernel, {'project': block[-1]},...  42.9 us

profile of v1, /device:TPU:0, one launch (start us, length us, event | category | flops | bytes accessed | tf_op | source)
XLA Modules:
  0.0 324.0 jit_solution(5840250156809205576)
XLA Ops:
  0.8 1.5 broadcast_add_fusion
  2.3 1.0 copy.60.code_ref.refs_8_
  3.3 3.1 multiply_sine_fusion
  6.7 0.7 fusion.1.project_hbm
  7.4 0.7 pad_maximum_fusion.upper_hbm
  8.1 102.9 %gather_attend.1 = (bf16[1024,768]{1,0:T(8,128)(2,1)}, bf16[1024,768]{1,0:T(8,128)(2,1)}, bf16[1024,768]{1,0:T(8,128)(2,1)}, bf16[1024,768]{1,0:T(8,128)(2,1)}, ...) custom-call(bf16[48,1280]{1,0:T(8,128)(2,1)} %fusion.1.project_hbm, ...), custom_call_target="tpu_custom_call" | custom-call | tf_op jit(solution)/shard_map/gather_attend/pallas_call | solution.py:751
  111.0 0.7 slice.39
  111.8 0.7 reshape_reshape.3.shift_ref
  112.6 75.3 %feed_forward.1 = (bf16[1024,768]{1,0:T(8,128)(2,1)}, bf16[1024,768]{1,0:T(8,128)(2,1)}, f32[6,768]{1,0:T(8,128)}, f32[1,3072]{1,0:T(1,128)}, bf16[8,128,768]{2,...) custom-call(bf16[1024,768]{1,0:T(8,128)(2,1)} %get-tuple-element.37.a_ref.refs_3_, ...), custom_call_target="tpu_custom_call" | custom-call | flops 32614907904 | bytes 31457280 | tf_op jit(solution)/shard_map/feed_forward/pallas_call | solution.py:1271
  188.4 1.4 reduce.15
  190.0 1.4 pad_maximum_fusion.1.refs_14_
  191.4 79.7 %back_scatter.1 = (bf16[1024,768]{1,0:T(8,128)(2,1)}, bf16[768,2560]{1,0:T(8,128)(2,1)}, f32[48,1920]{1,0:T(8,128)}, f32[48,1536]{1,0:T(8,128)}) custom-call(bf16[1024,768]{1,0:T(8,128)(2,1)} %get-tuple-element.43.refs_0_, bf16[1024,768]{1,0:T(8,128)(2,1)} %get-tuple-element.44.refs_1_, bf16[1024,768]{1,0:T(8,128)(2,1)} %get-tuple-element.45.refs_2_, ...), custom_call_target="tpu_custom_call" | custom-call | tf_op jit(solution)/shard_map/back_scatter/pallas_call | solution.py:960
  271.1 42.9 %scatter_last.1 = (f32[48,1280]{1,0:T(8,128)}, bf16[8,128,768]{2,1,0:T(8,128)(2,1)}) custom-call(bf16[16,48,2560]{2,1,0:T(8,128)(2,1)} %bitcast.38, bf16[8,128,768]{2,1,0:T(8,128)(2,1)} %bitcast.40), custom_call_target="tpu_custom_call" | custom-call | tf_op jit(solution)/shard_map/scatter_last/pallas_call | solution.py:1006
  314.0 1.1 slice.40
  315.1 0.7 copy.72
  315.8 0.7 slice_bitcast_fusion.1
  316.7 0.7 reshape.114
  317.3 0.8 slice_reduce_fusion
  318.1 0.7 copy.66
  318.8 0.7 slice.42
  320.2 1.1 copy.78
  321.3 0.8 copy-done.1
  322.1 1.1 copy.79
  323.3 0.7 copy.80
  (47 shorter events, 1.9 us)
Async XLA Ops:
  0.7 5.7 %copy-start.5 = (bf16[48,3,384]{2,0,1:T(8,128)(2,1)S(1)}, bf16[48,3,384]{2,0,1:T(8,128)(2,1)}, u32[]{:S(2)}) copy-start(bf16[48,3,384]{2,0,1:T(8,128)(2,1)} %param.17) | copy-start | bytes 331780
  0.7 5.7 %copy-start.15 = (bf16[192]{0:T(256)(128)(2,1)S(1)}, bf16[192]{0:T(256)(128)(2,1)}, u32[]{:S(2)}) copy-start(bf16[192]{0:T(256)(128)(2,1)} %param.23) | copy-start | bytes 1156
  0.7 5.8 %copy-start.9 = (bf16[48]{0:T(256)(128)(2,1)S(1)}, bf16[48]{0:T(256)(128)(2,1)}, u32[]{:S(2)}) copy-start(bf16[48]{0:T(256)(128)(2,1)} %param.22) | copy-start | bytes 292
  0.7 5.8 %copy-start.10 = (bf16[48]{0:T(256)(128)(2,1)S(1)}, bf16[48]{0:T(256)(128)(2,1)}, u32[]{:S(2)}) copy-start(bf16[48]{0:T(256)(128)(2,1)} %param.24) | copy-start | bytes 292
  0.7 5.8 %copy-start.11 = (bf16[48]{0:T(256)(128)(2,1)S(1)}, bf16[48]{0:T(256)(128)(2,1)}, u32[]{:S(2)}) copy-start(bf16[48]{0:T(256)(128)(2,1)} %param.25) | copy-start | bytes 292
  0.7 5.8 %copy-start.12 = (bf16[48]{0:T(256)(128)(2,1)S(1)}, bf16[48]{0:T(256)(128)(2,1)}, u32[]{:S(2)}) copy-start(bf16[48]{0:T(256)(128)(2,1)} %param.26) | copy-start | bytes 292
  0.7 5.8 %copy-start.13 = (bf16[48]{0:T(256)(128)(2,1)S(1)}, bf16[48]{0:T(256)(128)(2,1)}, u32[]{:S(2)}) copy-start(bf16[48]{0:T(256)(128)(2,1)} %param.27) | copy-start | bytes 292
  0.7 5.8 %copy-start.14 = (bf16[48]{0:T(256)(128)(2,1)S(1)}, bf16[48]{0:T(256)(128)(2,1)}, u32[]{:S(2)}) copy-start(bf16[48]{0:T(256)(128)(2,1)} %param.28) | copy-start | bytes 292
  0.7 5.8 %copy-start.8 = (bf16[3,48]{1,0:T(4,128)(2,1)S(1)}, bf16[3,48]{1,0:T(4,128)(2,1)}, u32[]{:S(2)}) copy-start(bf16[3,48]{1,0:T(4,128)(2,1)} %param.21) | copy-start | bytes 868
  0.7 6.6 %copy-start.7 = (bf16[384,48]{0,1:T(8,128)(2,1)S(1)}, bf16[384,48]{0,1:T(8,128)(2,1)}, u32[]{:S(2)}) copy-start(bf16[384,48]{0,1:T(8,128)(2,1)} %param.18) | copy-start | bytes 110596
  0.8 6.6 %copy-start.4 = (bf16[48,1536]{1,0:T(8,128)(2,1)S(1)}, bf16[48,1536]{1,0:T(8,128)(2,1)}, u32[]{:S(2)}) copy-start(bf16[48,1536]{1,0:T(8,128)(2,1)} %param.19) | copy-start | bytes 442372
  2.3 5.8 %copy-start.6 = (s32[1,1024]{1,0:T(1,128)}, s32[1,1024]{1,0:T(1,128)S(1)}, u32[]{:S(2)}) copy-start(s32[1,1024]{1,0:T(1,128)S(1)} %get-tuple-element.109.low_ref.refs_9_) | copy-start | bytes 12292
  271.1 47.7 %copy-start.2 = (f32[48,1920]{1,0:T(8,128)S(1)}, f32[48,1920]{1,0:T(8,128)}, u32[]{:S(2)}) copy-start(f32[48,1920]{1,0:T(8,128)} %get-tuple-element.58) | copy-start | bytes 1105924
  314.0 6.2 %copy-start = (bf16[8,128,768]{2,1,0:T(8,128)(2,1)S(1)}, bf16[8,128,768]{2,1,0:T(8,128)(2,1)}, u32[]{:S(2)}) copy-start(bf16[8,128,768]{2,1,0:T(8,128)(2,1)} %get-tuple-element.126) | copy-start | bytes 4718596
  320.2 2.0 copy-start.1
  322.1 1.1 copy-start.3
